TPU v7x, 32 devices: a whole 2x2x4 slice. The times are simulated.
32 devices in a mesh: row: 4 (over y, x), col: 8 (over z, core).
Axes of the slice: x: 2, y: 2, z: 4, core: 2. Of those that a mesh axis runs over, the one named last changes fastest.
Arguments:
- tiles: float32 [384, 1024, 128], P('row', 'col'), may hold values from -0.1875 to 0.1875
- tile_row: int32 [384, 8], P('row', 'col'), may hold values from 0 to 511
- tile_col: int32 [384, 8], P('row', 'col'), may hold values from 0 to 255
- tile_count: int32 [4, 8], P('row', 'col'), may hold values from 24 to 96, as said below
- cost: float32 [8, 32768], P('col', 'row'), may hold values from -6 to 6
- rhs: float32 [4, 65536], P('row', 'col'), may hold values from -6 to 6
- lower: float32 [8, 32768], P('col', 'row'), may hold values from -2 to -0.3
- upper: float32 [8, 32768], P('col', 'row'), may hold values from 0.3 to 2
- primal_start: float32 [8, 32768], P('col', 'row'), may hold values from -0.3 to 0.3
- dual_start: float32 [4, 65536], P('row', 'col'), may hold values from 0 to 1
Outputs:
- primal_mean: float32 [8, 32768], P('col', 'row')
- dual_mean: float32 [4, 65536], P('row', 'col')
- primal_last: float32 [8, 32768], P('col', 'row')
- dual_last: float32 [4, 65536], P('row', 'col')
Inputs may be any that keep to these rules, and one draw needn't show every extreme that they name: `tile_count`: live tiles of each device; some device holds 96.
All inputs are finite; a program needn't handle non-finite values.
Results may differ from a plain program's by a relative error of at most 0.0001.
Values sent between devices are 32-bit elements; how exact they have to be, the bound alone decides.
A program may use at most 64 MiB of HBM per device.

v0:
```python
import functools

import jax
import jax.numpy as jnp
from jax import lax
from jax.experimental import pallas as pl
from jax.experimental.pallas import tpu as pltpu
from jax.sharding import PartitionSpec as P

ITERS = 6
primal_step = 0.3
dual_step = 0.3
SUB = 8
CHUNKS = 3
TILE_PARTS = 4
UNROLL = 4
VMEM_BYTES = 62 * 1024 * 1024


def split_dot(hot, data):
    high = data.astype(jnp.bfloat16)
    rest = data - high.astype(jnp.float32)
    middle = rest.astype(jnp.bfloat16)
    low = (rest - middle.astype(jnp.float32)).astype(jnp.bfloat16)
    dot = functools.partial(jnp.dot, preferred_element_type=jnp.float32)
    return (dot(hot, low) + dot(hot, middle)) + dot(hot, high)


def pieces_of(data):
    high = data.astype(jnp.bfloat16).astype(jnp.float32)
    rest = data - high
    middle = rest.astype(jnp.bfloat16).astype(jnp.float32)
    return high, middle, rest - middle


def kernel(
    n_row, n_col,
    tiles_hbm, tile_row, tile_col, tile_count, cost, rhs, lower, upper, primal_start, dual_start,
    primal_mean, dual_mean, primal_last, dual_last,
    tiles, plain, flipped, y_init, x_init, c_init, z_all, p_all, y_hot, x_hot, y_column, x_column,
    y_state, b_state, x_state, c_state, l_state, u_state, extrapolated, y_total, x_total,
    row_line, col_line, count_cell, tile_sem, in_sem, z_send, z_recv, p_send, p_recv, yi_send, yi_recv, xi_send, xi_recv, ci_send, ci_recv,
):
    slots = tile_row.shape[1]
    sy = rhs.shape[0]
    sx = cost.shape[0]
    row = lax.axis_index("row")
    col = lax.axis_index("col")
    chips = n_col // 2
    chip = col // 2
    core = col % 2
    partner = chip * 2 + (1 - core)
    high_half = (chip * 2) // chips

    def chip_at(k):
        down = chips - 1 - k
        down = down - (chip - down + chips) // chips
        up = k + (k - chip + chips) // chips
        return (1 - high_half) * down + high_half * up

    def row_to(d):
        return (row + d) % n_row

    def row_from(d):
        return (row + n_row - d) % n_row

    local = [
        pltpu.make_async_copy(source, place, in_sem.at[i])
        for i, (source, place) in enumerate(
            [
                (primal_start, x_init.at[row, 0:sx]),
                (dual_start, y_init.at[col, 0:sy]),
                (rhs, y_init.at[col, sy : 2 * sy]),
                (cost, c_init.at[row, 0:sx]),
                (lower, c_init.at[row, sx : 2 * sx]),
                (upper, c_init.at[row, 2 * sx : 3 * sx]),
                (tile_row, row_line),
                (tile_col, col_line),
                (tile_count, count_cell),
            ]
        )
    ]
    for copy in local:
        copy.start()
    part = slots // TILE_PARTS
    tile_copies = [
        pltpu.make_async_copy(
            tiles_hbm.at[i * part : (i + 1) * part], tiles.at[i * part : (i + 1) * part], tile_sem.at[i]
        )
        for i in range(TILE_PARTS)
    ]
    for copy in tile_copies:
        copy.start()

    mesh_id = pl.DeviceIdType.MESH
    barrier = pltpu.get_barrier_semaphore()
    for d in range(1, n_row):
        pl.semaphore_signal(barrier, inc=1, device_id={"row": row_to(d)}, device_id_type=mesh_id)
    for k in range(chips - 1):
        pl.semaphore_signal(
            barrier, inc=1, device_id={"col": chip_at(k) * 2 + core}, device_id_type=mesh_id
        )
    pl.semaphore_signal(barrier, inc=1, device_id={"col": partner}, device_id_type=mesh_id)

    for copy in local[6:]:
        copy.wait()
    live = lax.broadcasted_iota(jnp.int32, (1, slots), 1) < count_cell[...]
    for ids, init, me, at in ((row_line, y_init, col, 2 * sy), (col_line, x_init, row, sx)):
        init[me, at : at + SUB, :] = jnp.full((SUB, 128), -1.0, jnp.float32)
        init[me, at : at + SUB, 0:slots] = jnp.broadcast_to(
            jnp.where(live, ids[...].astype(jnp.float32), -1.0), (SUB, slots)
        )

    def remote(place, send, recv, target):
        return pltpu.make_async_remote_copy(
            src_ref=place, dst_ref=place, send_sem=send, recv_sem=recv, device_id=target, device_id_type=mesh_id
        )

    def row_send(place_of, send, recv, c):
        for d in range(1, n_row):
            remote(place_of(row, c), send(d - 1, c), recv(d - 1, c), {"row": row_to(d)}).start()

    def row_wait(place_of, send, recv, chunks):
        for c in range(chunks):
            for d in range(1, n_row):
                remote(place_of(row_from(d), c), send(d - 1, c), recv(d - 1, c), {"row": row_to(d)}).wait_recv()
        for c in range(chunks):
            for d in range(1, n_row):
                remote(place_of(row, c), send(d - 1, c), recv(d - 1, c), {"row": row_to(d)}).wait_send()

    def col_send(place_of, send, recv, c):
        for k in range(chips - 1):
            there = chip_at(k)
            remote(place_of(col, c), send(there, c), recv(chip, c), {"col": there * 2 + core}).start()
        remote(place_of(col, c), send(chip, c), recv(chip, c), {"col": partner}).start()

    def col_wait(place_of, send, recv, chunks):
        order = [(c, k) for c in range(chunks) for k in reversed(range(chips - 1))]
        to_partner = {"col": partner}
        for c, k in order:
            there = chip_at(k)
            block = place_of(there * 2 + core, c)
            remote(block, send(there, c), recv(there, c), to_partner).wait_recv()
            remote(block, send(chips + there, c), recv(chips + there, c), to_partner).start()
        for c in range(chunks):
            remote(place_of(partner, c), send(chip, c), recv(chip, c), to_partner).wait_recv()
        for c, k in order:
            there = chip_at(k)
            block = place_of(there * 2 + 1 - core, c)
            remote(block, send(chips + there, c), recv(chips + there, c), to_partner).wait_recv()
        for c, k in order:
            there = chip_at(k)
            remote(place_of(col, c), send(there, c), recv(chip, c), to_partner).wait_send()
            block = place_of(there * 2 + core, c)
            remote(block, send(chips + there, c), recv(chips + there, c), to_partner).wait_send()
        for c in range(chunks):
            remote(place_of(col, c), send(chip, c), recv(chip, c), to_partner).wait_send()

    def whole(buffer, send, recv):
        return (lambda i, c: buffer.at[i], lambda k, c: send.at[k], lambda k, c: recv.at[k])

    def sliced(buffer, send, recv, now):
        size = slots // CHUNKS
        return (
            lambda i, c: buffer.at[now, i, c * size : (c + 1) * size],
            lambda k, c: send.at[now, k, c],
            lambda k, c: recv.at[now, k, c],
        )

    xi = whole(x_init, xi_send, xi_recv)
    ci = whole(c_init, ci_send, ci_recv)
    yi = whole(y_init, yi_send, yi_recv)
    local[0].wait()
    pl.semaphore_wait(barrier, (n_row - 1) + (chips - 1) + 1)
    row_send(*xi, 0)
    for copy in local[1:3]:
        copy.wait()
    col_send(*yi, 0)
    for copy in local[3:6]:
        copy.wait()
    row_send(*ci, 0)

    def pair_up(q, carry):
        for half in range(2):
            tile = tiles[2 * q + half]
            for out, data in ((plain, tile), (flipped, tile.T)):
                high = data.astype(jnp.bfloat16)
                out[q, 0:128, half * 128 : half * 128 + 128] = high
                out[q, 128:256, half * 128 : half * 128 + 128] = (
                    data - high.astype(jnp.float32)
                ).astype(jnp.bfloat16)
        return carry

    for i in range(TILE_PARTS):
        tile_copies[i].wait()
        lax.fori_loop(i * part // 2, (i + 1) * part // 2, pair_up, 0, unroll=2)

    def column_of(init, i, at):
        return init[i, at : at + SUB, :].T[:slots, 0:1]

    def own_ids(init, me, at):
        ids = column_of(init, me, at)
        return jnp.where(ids < 0.0, -2.0, ids)

    def hot_of(ids, first, share, column, hot, init, at, n):
        for i in range(n):
            column[i * slots : (i + 1) * slots, :] = jnp.broadcast_to(column_of(init, i, at), (slots, 128))
        wide = column[...].T[0:1, :]
        own = first + lax.broadcasted_iota(jnp.int32, (share, 1), 0)
        hot[0:slots, :] = jnp.where(ids == wide, 1.0, 0.0).astype(jnp.bfloat16)
        hot[slots : slots + share, :] = jnp.where(own.astype(jnp.float32) == wide, 1.0, 0.0).astype(jnp.bfloat16)

    def pick_of(ids, blocks):
        lanes = lax.broadcasted_iota(jnp.int32, (slots, blocks), 1).astype(jnp.float32)
        return jnp.where(ids == lanes, 1.0, 0.0).astype(jnp.bfloat16)

    def place_state(state, pick, init, at, share, me, n):
        state[0:slots, :] = split_dot(pick, init[:, at : at + share, :].reshape(n * share, 128))
        state[slots : slots + share, :] = init[me, at : at + share, :]

    def products(pairs, vectors, out, send):
        line = lax.broadcasted_iota(jnp.int32, (SUB, 128), 0)
        per_chunk = slots // SUB // CHUNKS

        def group(g, carry):
            at = pl.multiple_of(g * SUB, SUB)
            left = jnp.concatenate(pieces_of(vectors[pl.ds(at, SUB), :]), axis=0).astype(jnp.bfloat16)
            left = jnp.concatenate([left, left], axis=1)
            result = jnp.zeros((SUB, 128), jnp.float32)
            for q in range(SUB // 2):
                both = jnp.dot(left, pairs[g * (SUB // 2) + q], preferred_element_type=jnp.float32)
                total = (both[2 * SUB :] + both[SUB : 2 * SUB]) + both[:SUB]
                result = jnp.where(line == 2 * q, total[:, :128], result)
                result = jnp.where(line == 2 * q + 1, total[:, 128:], result)
            out[pl.ds(at, SUB), :] = result
            return carry

        for c in range(CHUNKS):
            lax.fori_loop(c * per_chunk, (c + 1) * per_chunk, group, 0, unroll=UNROLL)
            send(c)

    def forward(now):
        z = sliced(z_all, z_send, z_recv, now)
        products(flipped, extrapolated, z_all.at[now, col], lambda c: col_send(*z, c))

    row_wait(*xi, 1)
    col_ids = own_ids(x_init, row, sx)
    x_pick = pick_of(col_ids, n_row * sx)
    place_state(x_state, x_pick, x_init, 0, sx, row, n_row)
    extrapolated[...] = x_state[0:slots, :]
    forward(0)

    hot_of(col_ids, row * sx, sx, x_column, x_hot, x_init, sx, n_row)
    row_wait(*ci, 1)
    place_state(c_state, x_pick, c_init, 0, sx, row, n_row)
    place_state(l_state, x_pick, c_init, sx, sx, row, n_row)
    place_state(u_state, x_pick, c_init, 2 * sx, sx, row, n_row)
    col_wait(*yi, 1)
    row_ids = own_ids(y_init, col, 2 * sy)
    y_pick = pick_of(row_ids, n_col * sy)
    place_state(y_state, y_pick, y_init, 0, sy, col, n_col)
    place_state(b_state, y_pick, y_init, sy, sy, col, n_col)
    hot_of(row_ids, col * sy, sy, y_column, y_hot, y_init, 2 * sy, n_col)
    y_total[...] = jnp.zeros_like(y_total)
    x_total[...] = jnp.zeros_like(x_total)

    def iteration(step, carry):
        now = step % 2
        z = sliced(z_all, z_send, z_recv, now)
        p = sliced(p_all, p_send, p_recv, now)
        col_wait(*z, CHUNKS)
        applied = split_dot(y_hot[...], z_all[now].reshape(n_col * slots, 128))
        y_new = jnp.maximum(y_state[...] + dual_step * (b_state[...] - applied), 0.0)
        y_state[...] = y_new
        products(plain, y_state, p_all.at[now, row], lambda c: row_send(*p, c))
        y_total[...] += y_new[slots:, :]
        row_wait(*p, CHUNKS)
        transposed = split_dot(x_hot[...], p_all[now].reshape(n_row * slots, 128))
        x_old = x_state[...]
        moved = x_old - primal_step * (c_state[...] - transposed)
        x_new = jnp.minimum(jnp.maximum(moved, l_state[...]), u_state[...])
        x_state[...] = x_new
        extrapolated[...] = 2.0 * x_new[:slots, :] - x_old[:slots, :]

        @pl.when(step < ITERS - 1)
        def _():
            forward(1 - now)

        x_total[...] += x_new[slots:, :]
        return carry

    lax.fori_loop(0, ITERS, iteration, 0)

    primal_last[...] = x_state[slots:, :]
    dual_last[...] = y_state[slots:, :]
    primal_mean[...] = x_total[...] / ITERS
    dual_mean[...] = y_total[...] / ITERS


def body(n_row, n_col, tiles, tile_row, tile_col, tile_count, cost, rhs, lower, upper, primal_start, dual_start):
    slots, bs = tiles.shape[0], tiles.shape[2]
    blocks = [a.reshape(-1, bs) for a in (cost, rhs, lower, upper, primal_start, dual_start)]
    sx, sy = blocks[0].shape[0], blocks[1].shape[0]
    f32 = jnp.float32
    chips = n_col // 2
    vmem = pl.BlockSpec(memory_space=pltpu.VMEM)
    hbm = pl.BlockSpec(memory_space=pltpu.HBM)
    dma = pltpu.SemaphoreType.DMA
    state = lambda share: pltpu.VMEM((slots + share, bs), f32)
    out = pl.pallas_call(
        functools.partial(kernel, n_row, n_col),
        out_shape=[jax.ShapeDtypeStruct((s, bs), f32) for s in (sx, sy, sx, sy)],
        in_specs=[hbm] * 10,
        out_specs=[vmem] * 4,
        scratch_shapes=[
            pltpu.VMEM(tiles.shape, f32),
            pltpu.VMEM((slots // 2, 2 * bs, 2 * bs), jnp.bfloat16),
            pltpu.VMEM((slots // 2, 2 * bs, 2 * bs), jnp.bfloat16),
            pltpu.VMEM((n_col, 2 * sy + SUB, bs), f32),
            pltpu.VMEM((n_row, sx + SUB, bs), f32),
            pltpu.VMEM((n_row, 3 * sx, bs), f32),
            pltpu.VMEM((2, n_col, slots, bs), f32),
            pltpu.VMEM((2, n_row, slots, bs), f32),
            pltpu.VMEM((slots + sy, n_col * slots), jnp.bfloat16),
            pltpu.VMEM((slots + sx, n_row * slots), jnp.bfloat16),
            pltpu.VMEM((n_col * slots, bs), f32),
            pltpu.VMEM((n_row * slots, bs), f32),
            state(sy), state(sy), state(sx), state(sx), state(sx), state(sx),
            pltpu.VMEM((slots, bs), f32),
            pltpu.VMEM((sy, bs), f32),
            pltpu.VMEM((sx, bs), f32),
            pltpu.VMEM((1, slots), jnp.int32), pltpu.VMEM((1, slots), jnp.int32), pltpu.VMEM((1, 1), jnp.int32),
            dma((TILE_PARTS,)), dma((9,)),
            dma((2, 2 * chips, CHUNKS)), dma((2, 2 * chips, CHUNKS)),
            dma((2, n_row, CHUNKS)), dma((2, n_row, CHUNKS)),
            dma((2 * chips,)), dma((2 * chips,)),
            dma((n_row,)), dma((n_row,)),
            dma((n_row,)), dma((n_row,)),
        ],
        compiler_params=pltpu.CompilerParams(
            collective_id=0, has_side_effects=True, vmem_limit_bytes=VMEM_BYTES
        ),
        name="pdhg",
    )(tiles, tile_row.reshape(1, slots), tile_col.reshape(1, slots), tile_count, *blocks)
    return tuple(a.reshape(1, -1) for a in out)


def solution(mesh):
    return jax.shard_map(
        functools.partial(body, mesh.shape["row"], mesh.shape["col"]),
        mesh=mesh,
        in_specs=(
            P("row", "col", None),
            P("row", "col"),
            P("row", "col"),
            P("row", "col"),
            P("col", "row"),
            P("row", "col"),
            P("col", "row"),
            P("col", "row"),
            P("col", "row"),
            P("row", "col"),
        ),
        out_specs=(P("col", "row"), P("row", "col"), P("col", "row"), P("row", "col")),
        check_vma=False,
    )
```

profile of v0, /device:TPU:0, one launch (start us, length us, event | category | flops | bytes accessed | tf_op | source)
XLA Modules:
  0.0 98.8 jit_solution(6576600605439256796)
XLA Ops:
  1.3 92.0 %pdhg.1 = (f32[64,128]{1,0:T(8,128)}, f32[64,128]{1,0:T(8,128)}, f32[64,128]{1,0:T(8,128)}, f32[64,128]{1,0:T(8,128)}) custom-call(f32[96,128,128]{2,1,0:T(8,128)} %tiles_hbm.1, s32[1,96]{1,0:T(1,128)} %bitcast.22, s32[1,96]{1,0:T(1,128)} %bitcast.23, s32[1,1]{1,0:T(1,128)S(6)} %copy.18.tile_count, f32[64,128]{1,0:T(8,128)} %bitcast.12, f32[64,128]{1,0:T(8,128)} %bitcast.13, ...), custom_call_target="tpu_custom_call" | custom-call | tf_op jit(solution)/shard_map/pdhg/pallas_call | solution.py:310
  93.3 1.4 %copy.19 = f32[1,8192]{1,0:T(1,128)} copy(f32[1,8192]{1,0:T(1,128)} %bitcast.21) | data formatting | bytes 65536
  94.6 1.4 %copy.20 = f32[1,8192]{1,0:T(1,128)} copy(f32[1,8192]{1,0:T(1,128)} %bitcast.20) | data formatting | bytes 65536
  96.0 1.4 %copy.21 = f32[1,8192]{1,0:T(1,128)} copy(f32[1,8192]{1,0:T(1,128)} %bitcast.19) | data formatting | bytes 65536
  97.4 1.4 %copy.22 = f32[1,8192]{1,0:T(1,128)} copy(f32[1,8192]{1,0:T(1,128)} %bitcast.18) | data formatting | bytes 65536
where the time goes:
time: 99.1 us; the launch traced here: 98.8 us
  Pallas kernels  92 us (93%)
  local copies, waits for them, and re-layouts  5.5 us (6%)
  between operations  1.29 us (1%)
    pallas_call x1, Pallas kernels, body(): pl.pallas_call(functools.partial(kernel, n_row, n_col), out_shape=[jax.Sh...  92 us
    unnamed x4, local copies, waits for them, and re-layouts  5.5 us

commit v1 on v0

v1 whole, which is shorter than its diff:
```python
import functools

import jax
import jax.numpy as jnp
from jax import lax
from jax.experimental import pallas as pl
from jax.experimental.pallas import tpu as pltpu
from jax.sharding import PartitionSpec as P

ITERS = 6
primal_step = 0.3
dual_step = 0.3
SUB = 8
CHUNKS = 3
TILE_PARTS = 4
UNROLL = 4
VMEM_BYTES = 48 * 1024 * 1024


def split_dot(hot, data):
    high = data.astype(jnp.bfloat16)
    rest = data - high.astype(jnp.float32)
    middle = rest.astype(jnp.bfloat16)
    low = (rest - middle.astype(jnp.float32)).astype(jnp.bfloat16)
    dot = functools.partial(jnp.dot, preferred_element_type=jnp.float32)
    return (dot(hot, low) + dot(hot, middle)) + dot(hot, high)


def pieces_of(data):
    high = data.astype(jnp.bfloat16).astype(jnp.float32)
    rest = data - high
    middle = rest.astype(jnp.bfloat16).astype(jnp.float32)
    return high, middle, rest - middle


def kernel(
    n_row, n_col,
    tiles_hbm, tile_row, tile_col, tile_count, cost, rhs, lower, upper, primal_start, dual_start,
    primal_mean, dual_mean, primal_last, dual_last,
    tiles, plain, flipped, y_init, x_init, b_init, c_init, z_all, p_all, y_hot, x_hot, y_column, x_column,
    y_state, b_state, x_state, c_state, l_state, u_state, extrapolated, y_total, x_total,
    row_line, col_line, count_cell, tile_sem, in_sem, z_send, z_recv, p_send, p_recv,
    yi_send, yi_recv, bi_send, bi_recv, xi_send, xi_recv, ci_send, ci_recv,
):
    slots = tile_row.shape[1]
    size = slots // CHUNKS
    sy = rhs.shape[0]
    sx = cost.shape[0]
    row = lax.axis_index("row")
    col = lax.axis_index("col")
    chips = n_col // 2
    chip = col // 2
    core = col % 2
    partner = chip * 2 + (1 - core)
    high_half = (chip * 2) // chips

    def chip_at(k):
        down = chips - 1 - k
        down = down - (chip - down + chips) // chips
        up = k + (k - chip + chips) // chips
        return (1 - high_half) * down + high_half * up

    def row_to(d):
        return (row + d) % n_row

    def row_from(d):
        return (row + n_row - d) % n_row

    local = [
        pltpu.make_async_copy(source, place, in_sem.at[i])
        for i, (source, place) in enumerate(
            [
                (primal_start, x_init.at[row, 0:sx]),
                (dual_start, y_init.at[col, 0:sy]),
                (rhs, b_init.at[col]),
                (cost, c_init.at[row, 0:sx]),
                (lower, c_init.at[row, sx : 2 * sx]),
                (upper, c_init.at[row, 2 * sx : 3 * sx]),
                (tile_row, row_line),
                (tile_col, col_line),
                (tile_count, count_cell),
            ]
        )
    ]
    for copy in local:
        copy.start()
    part = slots // TILE_PARTS
    tile_copies = [
        pltpu.make_async_copy(
            tiles_hbm.at[i * part : (i + 1) * part], tiles.at[i * part : (i + 1) * part], tile_sem.at[i]
        )
        for i in range(TILE_PARTS)
    ]
    for copy in tile_copies:
        copy.start()

    mesh_id = pl.DeviceIdType.MESH
    barrier = pltpu.get_barrier_semaphore()
    for d in range(1, n_row):
        pl.semaphore_signal(barrier, inc=1, device_id={"row": row_to(d)}, device_id_type=mesh_id)
    for k in range(chips - 1):
        pl.semaphore_signal(
            barrier, inc=1, device_id={"col": chip_at(k) * 2 + core}, device_id_type=mesh_id
        )
    pl.semaphore_signal(barrier, inc=1, device_id={"col": partner}, device_id_type=mesh_id)

    for copy in local[6:]:
        copy.wait()
    live = lax.broadcasted_iota(jnp.int32, (1, slots), 1) < count_cell[...]
    for ids, init, me, at in ((row_line, y_init, col, sy), (col_line, x_init, row, sx)):
        init[me, at : at + SUB, :] = jnp.full((SUB, 128), -1.0, jnp.float32)
        init[me, at : at + SUB, 0:slots] = jnp.broadcast_to(
            jnp.where(live, ids[...].astype(jnp.float32), -1.0), (SUB, slots)
        )

    def remote(place, send, recv, target):
        return pltpu.make_async_remote_copy(
            src_ref=place, dst_ref=place, send_sem=send, recv_sem=recv, device_id=target, device_id_type=mesh_id
        )

    def row_send(place_of, send, recv, c):
        for d in range(1, n_row):
            remote(place_of(row, c), send(d - 1, c), recv(d - 1, c), {"row": row_to(d)}).start()

    def row_arrive(place_of, send, recv, c):
        for d in range(1, n_row):
            remote(place_of(row_from(d), c), send(d - 1, c), recv(d - 1, c), {"row": row_to(d)}).wait_recv()

    def row_sent(place_of, send, recv, c):
        for d in range(1, n_row):
            remote(place_of(row, c), send(d - 1, c), recv(d - 1, c), {"row": row_to(d)}).wait_send()

    to_partner = {"col": partner}

    def col_send(place_of, send, recv, c):
        for k in range(chips - 1):
            there = chip_at(k)
            remote(place_of(col, c), send(there, c), recv(chip, c), {"col": there * 2 + core}).start()
        remote(place_of(col, c), send(chip, c), recv(chip, c), to_partner).start()

    def col_arrive(place_of, send, recv, c):
        for k in reversed(range(chips - 1)):
            there = chip_at(k)
            block = place_of(there * 2 + core, c)
            remote(block, send(there, c), recv(there, c), to_partner).wait_recv()
            remote(block, send(chips + there, c), recv(chips + there, c), to_partner).start()

    def col_complete(place_of, send, recv, c):
        remote(place_of(partner, c), send(chip, c), recv(chip, c), to_partner).wait_recv()
        for k in reversed(range(chips - 1)):
            there = chip_at(k)
            block = place_of(there * 2 + 1 - core, c)
            remote(block, send(chips + there, c), recv(chips + there, c), to_partner).wait_recv()

    def col_sent(place_of, send, recv, c):
        for k in reversed(range(chips - 1)):
            there = chip_at(k)
            remote(place_of(col, c), send(there, c), recv(chip, c), to_partner).wait_send()
            block = place_of(there * 2 + core, c)
            remote(block, send(chips + there, c), recv(chips + there, c), to_partner).wait_send()
        remote(place_of(col, c), send(chip, c), recv(chip, c), to_partner).wait_send()

    def whole(buffer, send, recv):
        return (lambda i, c: buffer.at[i], lambda k, c: send.at[k], lambda k, c: recv.at[k])

    def sliced(buffer, send, recv, now):
        return (
            lambda i, c: buffer.at[now, c, i],
            lambda k, c: send.at[now, k, c],
            lambda k, c: recv.at[now, k, c],
        )

    xi = whole(x_init, xi_send, xi_recv)
    ci = whole(c_init, ci_send, ci_recv)
    yi = whole(y_init, yi_send, yi_recv)
    bi = whole(b_init, bi_send, bi_recv)
    local[0].wait()
    pl.semaphore_wait(barrier, (n_row - 1) + (chips - 1) + 1)
    row_send(*xi, 0)
    for copy in local[1:3]:
        copy.wait()
    y_init[col, 0:sy, :] = y_init[col, 0:sy, :] + dual_step * b_init[col]
    col_send(*yi, 0)

    def pair_up(q, carry):
        for half in range(2):
            tile = tiles[2 * q + half]
            for out, data in ((plain, tile), (flipped, tile.T)):
                high = data.astype(jnp.bfloat16)
                out[q, 0:128, half * 128 : half * 128 + 128] = high
                out[q, 128:256, half * 128 : half * 128 + 128] = (
                    data - high.astype(jnp.float32)
                ).astype(jnp.bfloat16)
        return carry

    for i in range(TILE_PARTS):
        tile_copies[i].wait()
        lax.fori_loop(i * part // 2, (i + 1) * part // 2, pair_up, 0, unroll=2)

    def column_of(init, i, at):
        return init[i, at : at + SUB, :].T[:slots, 0:1]

    def own_ids(init, me, at):
        ids = column_of(init, me, at)
        return jnp.where(ids < 0.0, -2.0, ids)

    def hot_of(ids, first, share, column, hot, init, at, n):
        for i in range(n):
            ids_of = jnp.broadcast_to(column_of(init, i, at), (slots, 128))
            for c in range(CHUNKS):
                start = (c * n + i) * size
                column[start : start + size, :] = ids_of[c * size : (c + 1) * size, :]
        wide_all = column[...].T[0:1, :]
        own = (first + lax.broadcasted_iota(jnp.int32, (share, 1), 0)).astype(jnp.float32)
        for c in range(CHUNKS):
            wide = wide_all[:, c * n * size : (c + 1) * n * size]
            hot[c, 0:slots, :] = jnp.where(ids == wide, 1.0, 0.0).astype(jnp.bfloat16)
            hot[c, slots : slots + share, :] = jnp.where(own == wide, 1.0, 0.0).astype(jnp.bfloat16)

    def pick_of(ids, blocks):
        lanes = lax.broadcasted_iota(jnp.int32, (slots, blocks), 1).astype(jnp.float32)
        return jnp.where(ids == lanes, 1.0, 0.0).astype(jnp.bfloat16)

    def place_state(state, pick, init, at, share, me, n):
        state[0:slots, :] = split_dot(pick, init[:, at : at + share, :].reshape(n * share, 128))
        state[slots : slots + share, :] = init[me, at : at + share, :]

    def products(pairs, vectors, out, send):
        line = lax.broadcasted_iota(jnp.int32, (SUB, 128), 0)
        per_chunk = slots // SUB // CHUNKS

        for c in range(CHUNKS):
            place = out(c)

            def group(i, carry):
                g = c * per_chunk + i
                at = pl.multiple_of(g * SUB, SUB)
                left = jnp.concatenate(pieces_of(vectors[pl.ds(at, SUB), :]), axis=0).astype(jnp.bfloat16)
                left = jnp.concatenate([left, left], axis=1)
                result = jnp.zeros((SUB, 128), jnp.float32)
                for q in range(SUB // 2):
                    both = jnp.dot(left, pairs[g * (SUB // 2) + q], preferred_element_type=jnp.float32)
                    total = (both[2 * SUB :] + both[SUB : 2 * SUB]) + both[:SUB]
                    result = jnp.where(line == 2 * q, total[:, :128], result)
                    result = jnp.where(line == 2 * q + 1, total[:, 128:], result)
                place[pl.ds(pl.multiple_of(i * SUB, SUB), SUB), :] = result
                return carry

            lax.fori_loop(0, per_chunk, group, 0, unroll=UNROLL)
            send(c)

    def forward(now):
        z = sliced(z_all, z_send, z_recv, now)
        products(
            flipped, extrapolated, lambda c: z_all.at[now, c, col], lambda c: col_send(*z, c)
        )

    row_arrive(*xi, 0)
    col_ids = own_ids(x_init, row, sx)
    x_pick = pick_of(col_ids, n_row * sx)
    place_state(x_state, x_pick, x_init, 0, sx, row, n_row)
    extrapolated[...] = x_state[0:slots, :]
    forward(0)
    for copy in local[3:6]:
        copy.wait()
    row_send(*ci, 0)
    hot_of(col_ids, row * sx, sx, x_column, x_hot, x_init, sx, n_row)
    col_arrive(*yi, 0)
    col_complete(*yi, 0)
    row_ids = own_ids(y_init, col, sy)
    y_pick = pick_of(row_ids, n_col * sy)
    place_state(y_state, y_pick, y_init, 0, sy, col, n_col)
    hot_of(row_ids, col * sy, sy, y_column, y_hot, y_init, sy, n_col)
    y_total[...] = jnp.zeros_like(y_total)
    x_total[...] = jnp.zeros_like(x_total)

    last_chunk = CHUNKS - 1

    def gather_of(buffer, now, c, n):
        return buffer[now, c].reshape(n * size, 128)

    def iteration(step, now, first, final):
        z = sliced(z_all, z_send, z_recv, now)
        p = sliced(p_all, p_send, p_recv, now)
        summed = None
        for c in range(CHUNKS):
            col_arrive(*z, c)
            if c > 0:
                col_complete(*z, c - 1)
                term = split_dot(y_hot[c - 1], gather_of(z_all, now, c - 1, n_col))
                summed = term if summed is None else summed + term
        col_complete(*z, last_chunk)

        def new_y(rows, applied):
            old = y_state[rows, :]
            if first:
                return jnp.maximum(old - dual_step * applied, 0.0)
            return jnp.maximum(old + dual_step * (b_state[rows, :] - applied), 0.0)

        z_last = gather_of(z_all, now, last_chunk, n_col)
        mine = slice(0, slots)
        shared = slice(slots, slots + sy)
        y_state[mine, :] = new_y(mine, summed[mine] + split_dot(y_hot[last_chunk, mine, :], z_last))
        if first:
            col_send(*bi, 0)
        products(plain, y_state, lambda c: p_all.at[now, c, row], lambda c: row_send(*p, c))
        y_new = new_y(shared, summed[shared] + split_dot(y_hot[last_chunk, shared, :], z_last))
        y_state[shared, :] = y_new
        if final:
            dual_last[...] = y_new
            dual_mean[...] = (y_total[...] + y_new) / ITERS
        else:
            y_total[...] += y_new
        for c in range(CHUNKS):
            col_sent(*z, c)
        if first:
            row_sent(*xi, 0)
            col_sent(*yi, 0)
            row_arrive(*ci, 0)
            row_sent(*ci, 0)
            place_state(c_state, x_pick, c_init, 0, sx, row, n_row)
            place_state(l_state, x_pick, c_init, sx, sx, row, n_row)
            place_state(u_state, x_pick, c_init, 2 * sx, sx, row, n_row)

        def new_x(rows, transposed):
            moved = x_state[rows, :] - primal_step * (c_state[rows, :] - transposed)
            return jnp.minimum(jnp.maximum(moved, l_state[rows, :]), u_state[rows, :])

        mine = slice(0, slots)
        shared = slice(slots, slots + sx)
        needed = slice(slots if final else 0, slots + sx)
        summed = None
        for c in range(CHUNKS):
            row_arrive(*p, c)
            if c < last_chunk:
                term = split_dot(x_hot[c, needed, :], gather_of(p_all, now, c, n_row))
                summed = term if summed is None else summed + term
        p_last = gather_of(p_all, now, last_chunk, n_row)
        if not final:
            x_old = x_state[mine, :]
            x_new = new_x(mine, summed[mine] + split_dot(x_hot[last_chunk, mine, :], p_last))
            x_state[mine, :] = x_new
            extrapolated[...] = 2.0 * x_new - x_old
            forward(1 - now)
            summed = summed[shared]
        x_new = new_x(shared, summed + split_dot(x_hot[last_chunk, shared, :], p_last))
        if final:
            primal_last[...] = x_new
            primal_mean[...] = (x_total[...] + x_new) / ITERS
        else:
            x_state[shared, :] = x_new
            x_total[...] += x_new
        for c in range(CHUNKS):
            row_sent(*p, c)
        if first:
            col_arrive(*bi, 0)
            col_complete(*bi, 0)
            place_state(b_state, y_pick, b_init, 0, sy, col, n_col)
            col_sent(*bi, 0)

    iteration(0, 0, True, False)

    def middle(step, carry):
        iteration(step, step % 2, False, False)
        return carry

    lax.fori_loop(1, ITERS - 1, middle, 0)
    iteration(ITERS - 1, (ITERS - 1) % 2, False, True)


def in_hbm(array):
    return pltpu.with_memory_space_constraint(array, pltpu.HBM)


def finish(*refs):
    sems = refs[-1]
    copies = [
        pltpu.make_async_copy(source, place, sems.at[i])
        for i, (source, place) in enumerate(zip(refs[:4], refs[4:8]))
    ]
    for copy in copies:
        copy.start()
    for copy in copies:
        copy.wait()


def body(n_row, n_col, tiles, tile_row, tile_col, tile_count, cost, rhs, lower, upper, primal_start, dual_start):
    slots, bs = tiles.shape[0], tiles.shape[2]
    blocks = [a.reshape(-1, bs) for a in (cost, rhs, lower, upper, primal_start, dual_start)]
    sx, sy = blocks[0].shape[0], blocks[1].shape[0]
    f32 = jnp.float32
    chips = n_col // 2
    size = slots // CHUNKS
    vmem = pl.BlockSpec(memory_space=pltpu.VMEM)
    hbm = pl.BlockSpec(memory_space=pltpu.HBM)
    dma = pltpu.SemaphoreType.DMA
    state = lambda share: pltpu.VMEM((slots + share, bs), f32)
    shapes = [jax.ShapeDtypeStruct((s, bs), f32) for s in (sx, sy, sx, sy)]
    out = pl.pallas_call(
        functools.partial(kernel, n_row, n_col),
        out_shape=shapes,
        in_specs=[hbm] * 10,
        out_specs=[vmem] * 4,
        scratch_shapes=[
            pltpu.VMEM(tiles.shape, f32),
            pltpu.VMEM((slots // 2, 2 * bs, 2 * bs), jnp.bfloat16),
            pltpu.VMEM((slots // 2, 2 * bs, 2 * bs), jnp.bfloat16),
            pltpu.VMEM((n_col, sy + SUB, bs), f32),
            pltpu.VMEM((n_row, sx + SUB, bs), f32),
            pltpu.VMEM((n_col, sy, bs), f32),
            pltpu.VMEM((n_row, 3 * sx, bs), f32),
            pltpu.VMEM((2, CHUNKS, n_col, size, bs), f32),
            pltpu.VMEM((2, CHUNKS, n_row, size, bs), f32),
            pltpu.VMEM((CHUNKS, slots + sy, n_col * size), jnp.bfloat16),
            pltpu.VMEM((CHUNKS, slots + sx, n_row * size), jnp.bfloat16),
            pltpu.VMEM((n_col * slots, bs), f32),
            pltpu.VMEM((n_row * slots, bs), f32),
            state(sy), state(sy), state(sx), state(sx), state(sx), state(sx),
            pltpu.VMEM((slots, bs), f32),
            pltpu.VMEM((sy, bs), f32),
            pltpu.VMEM((sx, bs), f32),
            pltpu.VMEM((1, slots), jnp.int32), pltpu.VMEM((1, slots), jnp.int32), pltpu.VMEM((1, 1), jnp.int32),
            dma((TILE_PARTS,)), dma((9,)),
            dma((2, 2 * chips, CHUNKS)), dma((2, 2 * chips, CHUNKS)),
            dma((2, n_row, CHUNKS)), dma((2, n_row, CHUNKS)),
            dma((2 * chips,)), dma((2 * chips,)),
            dma((2 * chips,)), dma((2 * chips,)),
            dma((n_row,)), dma((n_row,)),
            dma((n_row,)), dma((n_row,)),
        ],
        compiler_params=pltpu.CompilerParams(
            collective_id=0, has_side_effects=True, vmem_limit_bytes=VMEM_BYTES
        ),
        name="pdhg",
    )(tiles, in_hbm(tile_row.reshape(1, slots)), in_hbm(tile_col.reshape(1, slots)), tile_count, *map(in_hbm, blocks))
    out = pl.pallas_call(
        finish,
        out_shape=shapes,
        in_specs=[vmem] * 4,
        out_specs=[hbm] * 4,
        scratch_shapes=[dma((4,))],
        compiler_params=pltpu.CompilerParams(vmem_limit_bytes=1024 * 1024),
        name="finish",
    )(*out)
    return tuple(a.reshape(1, -1) for a in out)


def solution(mesh):
    return jax.shard_map(
        functools.partial(body, mesh.shape["row"], mesh.shape["col"]),
        mesh=mesh,
        in_specs=(
            P("row", "col", None),
            P("row", "col"),
            P("row", "col"),
            P("row", "col"),
            P("col", "row"),
            P("row", "col"),
            P("col", "row"),
            P("col", "row"),
            P("col", "row"),
            P("row", "col"),
        ),
        out_specs=(P("col", "row"), P("row", "col"), P("col", "row"), P("row", "col")),
        check_vma=False,
    )
```

time: 99.1 us -> 89.2 us (0.900)
  local copies, waits for them, and re-layouts: 5.5 us -> 0 us
  Pallas kernels: 92 us -> 87.7 us
    unnamed x4 -> x0, local copies, waits for them, and re-layouts: 5.5 us -> none
    pallas_call x1 -> x2, Pallas kernels: 92 us -> 87.7 us  [the longest x1 87 us: body(): pl.pallas_call(functools.partial(kernel, n_row, n_col), out_shape=shapes,...]
where the time goes in v1:
time: 89.2 us; the launch traced here: 89 us
  Pallas kernels  87.7 us (98%)
  between operations  1.29 us (1%)
    pallas_call x1, Pallas kernels, body(): pl.pallas_call(functools.partial(kernel, n_row, n_col), out_shape=shapes,...  87 us

profile of v1, /device:TPU:0, one launch (start us, length us, event | category | flops | bytes accessed | tf_op | source)
XLA Modules:
  0.0 89.0 jit_solution(327928496751444391)
XLA Ops:
  1.3 87.0 %pdhg.1 = (f32[64,128]{1,0:T(8,128)S(1)}, f32[64,128]{1,0:T(8,128)S(1)}, f32[64,128]{1,0:T(8,128)S(1)}, f32[64,128]{1,0:T(8,128)S(1)}) custom-call(f32[96,128,128]{2,1,0:T(8,128)} %tiles_hbm.1, s32[1,96]{1,0:T(1,128)} %bitcast.18, s32[1,96]{1,0:T(1,128)} %bitcast.19, s32[1,1]{1,0:T(1,128)S(6)} %copy.14.tile_count, f32[64,128]{1,0:T(8,128)} %bitcast.12, ...), custom_call_target="tpu_custom_call" | custom-call | tf_op jit(solution)/shard_map/pdhg/pallas_call | solution.py:399
  88.3 0.7 finish.1

commit v2 on v1

--- a/solution.py
+++ b/solution.py
@@ -11,9 +11,9 @@
 primal_step = 0.3
 dual_step = 0.3
 SUB = 8
-CHUNKS = 3
+SHARES = (1, 2, 3)
+CHUNKS = len(SHARES)
 TILE_PARTS = 4
-UNROLL = 4
 VMEM_BYTES = 48 * 1024 * 1024
 
 
@@ -26,11 +26,21 @@
     return (dot(hot, low) + dot(hot, middle)) + dot(hot, high)
 
 
+def sum_dot(hot, data):
+    high = data.astype(jnp.bfloat16)
+    rest = (data - high.astype(jnp.float32)).astype(jnp.bfloat16)
+    dot = functools.partial(jnp.dot, preferred_element_type=jnp.float32)
+    return dot(hot, rest) + dot(hot, high)
+
+
+def edges_of(slots):
+    return [slots * k // sum(SHARES) // SUB * SUB for k in (sum(SHARES[:i]) for i in range(CHUNKS + 1))]
+
+
 def pieces_of(data):
     high = data.astype(jnp.bfloat16).astype(jnp.float32)
     rest = data - high
-    middle = rest.astype(jnp.bfloat16).astype(jnp.float32)
-    return high, middle, rest - middle
+    return high, rest
 
 
 def kernel(
@@ -43,7 +53,7 @@
     yi_send, yi_recv, bi_send, bi_recv, xi_send, xi_recv, ci_send, ci_recv,
 ):
     slots = tile_row.shape[1]
-    size = slots // CHUNKS
+    edges = edges_of(slots)
     sy = rhs.shape[0]
     sx = cost.shape[0]
     row = lax.axis_index("row")
@@ -61,9 +71,13 @@
         return (1 - high_half) * down + high_half * up
 
     def row_to(d):
+        if n_row == 4:
+            return (n_row - 1 - row, (row + 2) % n_row, row + 1 - 2 * (row % 2))[d - 1]
         return (row + d) % n_row
 
     def row_from(d):
+        if n_row == 4:
+            return row_to(d)
         return (row + n_row - d) % n_row
 
     local = [
@@ -163,9 +177,13 @@
     def whole(buffer, send, recv):
         return (lambda i, c: buffer.at[i], lambda k, c: send.at[k], lambda k, c: recv.at[k])
 
-    def sliced(buffer, send, recv, now):
+    def span(buffer, now, n, i, c):
+        size = edges[c + 1] - edges[c]
+        return buffer.at[now, pl.ds(pl.multiple_of(n * edges[c] + i * size, SUB), size)]
+
+    def sliced(buffer, send, recv, now, n):
         return (
-            lambda i, c: buffer.at[now, c, i],
+            lambda i, c: span(buffer, now, n, i, c),
             lambda k, c: send.at[now, k, c],
             lambda k, c: recv.at[now, k, c],
         )
@@ -208,14 +226,16 @@
         for i in range(n):
             ids_of = jnp.broadcast_to(column_of(init, i, at), (slots, 128))
             for c in range(CHUNKS):
-                start = (c * n + i) * size
-                column[start : start + size, :] = ids_of[c * size : (c + 1) * size, :]
+                size = edges[c + 1] - edges[c]
+                start = n * edges[c] + i * size
+                column[start : start + size, :] = ids_of[edges[c] : edges[c + 1], :]
         wide_all = column[...].T[0:1, :]
         own = (first + lax.broadcasted_iota(jnp.int32, (share, 1), 0)).astype(jnp.float32)
         for c in range(CHUNKS):
-            wide = wide_all[:, c * n * size : (c + 1) * n * size]
-            hot[c, 0:slots, :] = jnp.where(ids == wide, 1.0, 0.0).astype(jnp.bfloat16)
-            hot[c, slots : slots + share, :] = jnp.where(own == wide, 1.0, 0.0).astype(jnp.bfloat16)
+            wide = wide_all[:, n * edges[c] : n * edges[c + 1]]
+            width = n * (edges[c + 1] - edges[c])
+            hot[c, 0:slots, 0:width] = jnp.where(ids == wide, 1.0, 0.0).astype(jnp.bfloat16)
+            hot[c, slots : slots + share, 0:width] = jnp.where(own == wide, 1.0, 0.0).astype(jnp.bfloat16)
 
     def pick_of(ids, blocks):
         lanes = lax.broadcasted_iota(jnp.int32, (slots, blocks), 1).astype(jnp.float32)
@@ -227,32 +247,31 @@
 
     def products(pairs, vectors, out, send):
         line = lax.broadcasted_iota(jnp.int32, (SUB, 128), 0)
-        per_chunk = slots // SUB // CHUNKS
 
         for c in range(CHUNKS):
             place = out(c)
 
             def group(i, carry):
-                g = c * per_chunk + i
+                g = edges[c] // SUB + i
                 at = pl.multiple_of(g * SUB, SUB)
                 left = jnp.concatenate(pieces_of(vectors[pl.ds(at, SUB), :]), axis=0).astype(jnp.bfloat16)
                 left = jnp.concatenate([left, left], axis=1)
                 result = jnp.zeros((SUB, 128), jnp.float32)
                 for q in range(SUB // 2):
                     both = jnp.dot(left, pairs[g * (SUB // 2) + q], preferred_element_type=jnp.float32)
-                    total = (both[2 * SUB :] + both[SUB : 2 * SUB]) + both[:SUB]
+                    total = both[SUB:] + both[:SUB]
                     result = jnp.where(line == 2 * q, total[:, :128], result)
                     result = jnp.where(line == 2 * q + 1, total[:, 128:], result)
                 place[pl.ds(pl.multiple_of(i * SUB, SUB), SUB), :] = result
                 return carry
 
-            lax.fori_loop(0, per_chunk, group, 0, unroll=UNROLL)
+            lax.fori_loop(0, (edges[c + 1] - edges[c]) // SUB, group, 0, unroll=True)
             send(c)
 
     def forward(now):
-        z = sliced(z_all, z_send, z_recv, now)
+        z = sliced(z_all, z_send, z_recv, now, n_col)
         products(
-            flipped, extrapolated, lambda c: z_all.at[now, c, col], lambda c: col_send(*z, c)
+            flipped, extrapolated, lambda c: span(z_all, now, n_col, col, c), lambda c: col_send(*z, c)
         )
 
     row_arrive(*xi, 0)
@@ -277,17 +296,20 @@
     last_chunk = CHUNKS - 1
 
     def gather_of(buffer, now, c, n):
-        return buffer[now, c].reshape(n * size, 128)
+        return buffer[now, n * edges[c] : n * edges[c + 1], :]
+
+    def hot_at(hot, c, rows, n):
+        return hot[c, rows, 0 : n * (edges[c + 1] - edges[c])]
 
     def iteration(step, now, first, final):
-        z = sliced(z_all, z_send, z_recv, now)
-        p = sliced(p_all, p_send, p_recv, now)
+        z = sliced(z_all, z_send, z_recv, now, n_col)
+        p = sliced(p_all, p_send, p_recv, now, n_row)
         summed = None
         for c in range(CHUNKS):
             col_arrive(*z, c)
             if c > 0:
                 col_complete(*z, c - 1)
-                term = split_dot(y_hot[c - 1], gather_of(z_all, now, c - 1, n_col))
+                term = sum_dot(hot_at(y_hot, c - 1, slice(None), n_col), gather_of(z_all, now, c - 1, n_col))
                 summed = term if summed is None else summed + term
         col_complete(*z, last_chunk)
 
@@ -300,11 +322,11 @@
         z_last = gather_of(z_all, now, last_chunk, n_col)
         mine = slice(0, slots)
         shared = slice(slots, slots + sy)
-        y_state[mine, :] = new_y(mine, summed[mine] + split_dot(y_hot[last_chunk, mine, :], z_last))
+        y_state[mine, :] = new_y(mine, summed[mine] + sum_dot(hot_at(y_hot, last_chunk, mine, n_col), z_last))
         if first:
             col_send(*bi, 0)
-        products(plain, y_state, lambda c: p_all.at[now, c, row], lambda c: row_send(*p, c))
-        y_new = new_y(shared, summed[shared] + split_dot(y_hot[last_chunk, shared, :], z_last))
+        products(plain, y_state, lambda c: span(p_all, now, n_row, row, c), lambda c: row_send(*p, c))
+        y_new = new_y(shared, summed[shared] + sum_dot(hot_at(y_hot, last_chunk, shared, n_col), z_last))
         y_state[shared, :] = y_new
         if final:
             dual_last[...] = y_new
@@ -333,17 +355,17 @@
         for c in range(CHUNKS):
             row_arrive(*p, c)
             if c < last_chunk:
-                term = split_dot(x_hot[c, needed, :], gather_of(p_all, now, c, n_row))
+                term = sum_dot(hot_at(x_hot, c, needed, n_row), gather_of(p_all, now, c, n_row))
                 summed = term if summed is None else summed + term
         p_last = gather_of(p_all, now, last_chunk, n_row)
         if not final:
             x_old = x_state[mine, :]
-            x_new = new_x(mine, summed[mine] + split_dot(x_hot[last_chunk, mine, :], p_last))
+            x_new = new_x(mine, summed[mine] + sum_dot(hot_at(x_hot, last_chunk, mine, n_row), p_last))
             x_state[mine, :] = x_new
             extrapolated[...] = 2.0 * x_new - x_old
             forward(1 - now)
             summed = summed[shared]
-        x_new = new_x(shared, summed + split_dot(x_hot[last_chunk, shared, :], p_last))
+        x_new = new_x(shared, summed + sum_dot(hot_at(x_hot, last_chunk, shared, n_row), p_last))
         if final:
             primal_last[...] = x_new
             primal_mean[...] = (x_total[...] + x_new) / ITERS
@@ -390,7 +412,8 @@
     sx, sy = blocks[0].shape[0], blocks[1].shape[0]
     f32 = jnp.float32
     chips = n_col // 2
-    size = slots // CHUNKS
+    edges = edges_of(slots)
+    largest = max(b - a for a, b in zip(edges, edges[1:]))
     vmem = pl.BlockSpec(memory_space=pltpu.VMEM)
     hbm = pl.BlockSpec(memory_space=pltpu.HBM)
     dma = pltpu.SemaphoreType.DMA
@@ -409,10 +432,10 @@
             pltpu.VMEM((n_row, sx + SUB, bs), f32),
             pltpu.VMEM((n_col, sy, bs), f32),
             pltpu.VMEM((n_row, 3 * sx, bs), f32),
-            pltpu.VMEM((2, CHUNKS, n_col, size, bs), f32),
-            pltpu.VMEM((2, CHUNKS, n_row, size, bs), f32),
-            pltpu.VMEM((CHUNKS, slots + sy, n_col * size), jnp.bfloat16),
-            pltpu.VMEM((CHUNKS, slots + sx, n_row * size), jnp.bfloat16),
+            pltpu.VMEM((2, n_col * slots, bs), f32),
+            pltpu.VMEM((2, n_row * slots, bs), f32),
+            pltpu.VMEM((CHUNKS, slots + sy, n_col * largest), jnp.bfloat16),
+            pltpu.VMEM((CHUNKS, slots + sx, n_row * largest), jnp.bfloat16),
             pltpu.VMEM((n_col * slots, bs), f32),
             pltpu.VMEM((n_row * slots, bs), f32),
             state(sy), state(sy), state(sx), state(sx), state(sx), state(sx),

time: 89.2 us -> 86.3 us (0.967)
  Pallas kernels: 87.7 us -> 84.8 us
    pallas_call x1, Pallas kernels: 87 us -> 84.1 us  [body(): pl.pallas_call(functools.partial(kernel, n_row, n_col), out_shape=shapes,...]
where the time goes in v2:
time: 86.3 us; the launch traced here: 86.1 us
  Pallas kernels  84.8 us (98%)
  between operations  1.29 us (1%)
    pallas_call x1, Pallas kernels, body(): pl.pallas_call(functools.partial(kernel, n_row, n_col), out_shape=shapes,...  84.1 us

profile of v2, /device:TPU:0, one launch (start us, length us, event | category | flops | bytes accessed | tf_op | source)
XLA Modules:
  0.0 86.1 jit_solution(5343627602899732730)
XLA Ops:
  1.3 84.1 %pdhg.1 = (f32[64,128]{1,0:T(8,128)S(1)}, f32[64,128]{1,0:T(8,128)S(1)}, f32[64,128]{1,0:T(8,128)S(1)}, f32[64,128]{1,0:T(8,128)S(1)}) custom-call(f32[96,128,128]{2,1,0:T(8,128)} %tiles_hbm.1, s32[1,96]{1,0:T(1,128)} %bitcast.18, s32[1,96]{1,0:T(1,128)} %bitcast.19, s32[1,1]{1,0:T(1,128)S(6)} %copy.14.tile_count, f32[64,128]{1,0:T(8,128)} %bitcast.12, ...), custom_call_target="tpu_custom_call" | custom-call | tf_op jit(solution)/shard_map/pdhg/pallas_call | solution.py:422
  85.4 0.7 finish.1
